TPU v7x, 32 devices: a whole 2x2x4 slice. The times are simulated.
32 devices in a mesh: fsdp: 16 (over z, y, core), sp: 2 (over x).
Axes of the slice: x: 2, y: 2, z: 4, core: 2. Of those that a mesh axis runs over, the one named last changes fastest.
Arguments:
- latents: bfloat16 [32, 256, 768], P('fsdp', 'sp'), may hold values from -6 to 6
- condition: bfloat16 [32, 768], P('fsdp'), may hold values from -6 to 6
- cotangent: bfloat16 [32, 256, 768], P('fsdp', 'sp'), may hold values from -6 to 6
- w_ada: bfloat16 [768, 4608], P('fsdp'), may hold values from -0.21875 to 0.21875
- b_ada: bfloat16 [4608], P('fsdp'), may hold values from -3 to 3
- w_qkv: bfloat16 [768, 2304], P('fsdp'), may hold values from -0.21875 to 0.21875
- b_query: bfloat16 [768], P('fsdp'), may hold values from -3 to 3
- b_value: bfloat16 [768], P('fsdp'), may hold values from -3 to 3
- w_out: bfloat16 [768, 768], P('fsdp'), may hold values from -0.875 to 0.875
- b_out: bfloat16 [768], P('fsdp'), may hold values from -3 to 3
- w_up: bfloat16 [768, 3072], P('fsdp'), may hold values from -0.21875 to 0.21875
- b_up: bfloat16 [3072], P('fsdp'), may hold values from -3 to 3
- w_down: bfloat16 [3072, 768], P('fsdp'), may hold values from -0.109375 to 0.109375
- b_down: bfloat16 [768], P('fsdp'), may hold values from -3 to 3
Outputs:
- output: bfloat16 [32, 256, 768], P('fsdp', 'sp')
- grad_latents: float32 [32, 256, 768], P('fsdp', 'sp')
- grad_condition: float32 [32, 768], P('fsdp')
- grad_w_ada: float32 [768, 4608], P(('fsdp', 'sp'))
- grad_b_ada: float32 [4608], P(('fsdp', 'sp'))
- grad_w_qkv: float32 [768, 2304], P(('fsdp', 'sp'))
- grad_b_query: float32 [768], P(('fsdp', 'sp'))
- grad_b_value: float32 [768], P(('fsdp', 'sp'))
- grad_w_out: float32 [768, 768], P(('fsdp', 'sp'))
- grad_b_out: float32 [768], P(('fsdp', 'sp'))
- grad_w_up: float32 [768, 3072], P(('fsdp', 'sp'))
- grad_b_up: float32 [3072], P(('fsdp', 'sp'))
- grad_w_down: float32 [3072, 768], P(('fsdp', 'sp'))
- grad_b_down: float32 [768], P(('fsdp', 'sp'))
All inputs are finite; a program needn't handle non-finite values.
Results may differ from a plain program's by a relative error of at most 0.015.
The roundings to bfloat16 on the way count: a program that leaves them out, or rounds other values in their place, can miss the bound.
Values may be sent and summed in bfloat16 or wider, within the bound.
A program may use at most 256 MiB of HBM per device.

v0:
```python
import jax
import jax.numpy as jnp
from jax import lax
from jax.sharding import PartitionSpec as P

D = 768
H = 12
HD = 64
eps = 1e-06


def normalize(values):
    centered = values - jnp.mean(values, axis=-1, keepdims=True)
    inverse = lax.rsqrt(jnp.mean(centered * centered, axis=-1, keepdims=True) + eps)
    return (centered * inverse, inverse)


def norm_back(grad_in, normed, inverse):
    return inverse * (
        grad_in
        - jnp.mean(grad_in, axis=-1, keepdims=True)
        - normed * jnp.mean(grad_in * normed, axis=-1, keepdims=True)
    )


def gelu_tanh(values):
    return jax.nn.gelu(values, approximate=True)


def silu_back(values, grad_out):
    return jax.vjp(jax.nn.silu, values)[1](grad_out)[0]


def gelu_back(values, grad_out):
    return jax.vjp(gelu_tanh, values)[1](grad_out)[0]


LANES = 2048


def reduce_rows(grad):
    return lax.psum_scatter(
        grad.astype(jnp.bfloat16), ("fsdp", "sp"), scatter_dimension=0, tiled=True
    ).astype(jnp.float32)


def body(
    latents,
    condition,
    cotangent,
    w_ada,
    b_ada,
    w_qkv,
    b_query,
    b_value,
    w_out,
    b_out,
    w_up,
    b_up,
    w_down,
    b_down,
):
    f32 = jnp.float32
    bf16 = jnp.bfloat16
    fsdp_count = lax.axis_size("fsdp")
    sp_count = lax.axis_size("sp")
    owners = fsdp_count * sp_count
    fsdp_index = lax.axis_index("fsdp")
    sp_index = lax.axis_index("sp")
    owner_index = fsdp_index * sp_count + sp_index
    pair_latents = latents.shape[0]
    own_latents = pair_latents // sp_count
    latent_total = pair_latents * fsdp_count
    tokens_all = latents.shape[1] * sp_count
    scale_factor = HD ** (-0.5)
    small = [condition.reshape(-1), b_ada, b_query, b_value, b_out, b_up, b_down]
    width = sum((part.size for part in small))
    padded = -(-width // LANES) * LANES
    small.append(jnp.zeros((padded - width,), bf16))
    small_all = lax.all_gather(
        jnp.concatenate(small).reshape(1, padded // 128, 128), "fsdp", axis=0, tiled=True
    ).reshape(fsdp_count, padded)
    pieces = []
    start = 0
    for part in small[:-1]:
        pieces.append(small_all[:, start : start + part.size].reshape(-1))
        start = start + part.size
    cond_all, ada_bias, query_bias, value_bias, out_bias, up_bias, down_bias = pieces
    cond_all = cond_all.reshape(latent_total, D).astype(f32)
    silu_all = jax.nn.silu(cond_all)
    inputs = lax.all_to_all(latents, "sp", split_axis=0, concat_axis=1, tiled=True).astype(f32)
    grad_out = lax.all_to_all(cotangent, "sp", split_axis=0, concat_axis=1, tiled=True).astype(f32)
    ada_rows = w_ada.shape[0]
    silu_mine = lax.dynamic_index_in_dim(
        silu_all.astype(bf16).reshape(fsdp_count, sp_count, own_latents, D), sp_index, 1, False
    )
    silu_mine = lax.dynamic_index_in_dim(
        silu_mine.reshape(fsdp_count * own_latents, fsdp_count, ada_rows), fsdp_index, 1, False
    )
    mod_part = jnp.dot(silu_mine, w_ada, preferred_element_type=f32)
    mod_part = lax.all_to_all(
        mod_part.reshape(fsdp_count, own_latents * 6 * D),
        "fsdp",
        split_axis=0,
        concat_axis=0,
        tiled=True,
    )
    modulate = jnp.sum(mod_part, axis=0).reshape(own_latents, 6 * D) + ada_bias.astype(f32)
    mod_parts = modulate.reshape(own_latents, 6, 1, D)
    shift_one, scale_one, gate_one = (mod_parts[:, 0], mod_parts[:, 1], mod_parts[:, 2])
    shift_two, scale_two, gate_two = (mod_parts[:, 3], mod_parts[:, 4], mod_parts[:, 5])
    qkv_full = lax.all_gather(w_qkv, "fsdp", axis=0, tiled=True)
    out_full = lax.all_gather(w_out, "fsdp", axis=0, tiled=True)
    up_full = lax.all_gather(w_up, "fsdp", axis=0, tiled=True)
    down_full = lax.all_gather(w_down, "fsdp", axis=0, tiled=True)
    normed_one, inverse_one = normalize(inputs)
    attn_in = (normed_one * (1.0 + scale_one) + shift_one).astype(bf16)
    qkv_bias = jnp.concatenate([query_bias, jnp.zeros_like(query_bias), value_bias]).astype(f32)
    projected = (
        jnp.einsum("btd,de->bte", attn_in, qkv_full, preferred_element_type=f32) + qkv_bias
    ).astype(bf16)
    heads = projected.reshape(own_latents, tokens_all, 3, H, HD).transpose(2, 0, 3, 1, 4)
    queries, key_heads, value_heads = (heads[0], heads[1], heads[2])
    scores = (
        jnp.einsum("bhqd,bhkd->bhqk", queries, key_heads, preferred_element_type=f32) * scale_factor
    )
    log_total = jnp.log(jnp.sum(jnp.exp(scores), axis=-1, keepdims=True))
    soft_float = jnp.exp(scores - log_total)
    soft_half = soft_float.astype(bf16)
    mixed = jnp.einsum(
        "bhqk,bhkd->bhqd", soft_half, value_heads, preferred_element_type=f32
    ).astype(bf16)
    mixed_tokens = mixed.transpose(0, 2, 1, 3).reshape(own_latents, tokens_all, D)
    attn_proj = jnp.einsum(
        "btd,de->bte", mixed_tokens, out_full, preferred_element_type=f32
    ) + out_bias.astype(f32)
    residual = inputs + gate_one * attn_proj
    normed_two, inverse_two = normalize(residual)
    mlp_in = (normed_two * (1.0 + scale_two) + shift_two).astype(bf16)
    up_value = jnp.einsum(
        "btd,df->btf", mlp_in, up_full, preferred_element_type=f32
    ) + up_bias.astype(f32)
    activated = gelu_tanh(up_value).astype(bf16)
    down_value = jnp.einsum(
        "btf,fd->btd", activated, down_full, preferred_element_type=f32
    ) + down_bias.astype(f32)
    output = (residual + gate_two * down_value).astype(bf16)
    output = lax.all_to_all(output, "sp", split_axis=1, concat_axis=0, tiled=True)
    grad_gate_two = jnp.sum(grad_out * down_value, axis=1)
    grad_down = (grad_out * gate_two).astype(bf16)
    gw_down = jnp.einsum("btf,btd->fd", activated, grad_down, preferred_element_type=f32)
    own_down = reduce_rows(gw_down)
    gb_down = jnp.sum(grad_down.astype(f32), axis=(0, 1))
    grad_act = jnp.einsum("btd,fd->btf", grad_down, down_full, preferred_element_type=f32)
    grad_up = gelu_back(up_value, grad_act).astype(bf16)
    gw_up = jnp.einsum("btd,btf->df", mlp_in, grad_up, preferred_element_type=f32)
    own_up = reduce_rows(gw_up)
    gb_up = jnp.sum(grad_up.astype(f32), axis=(0, 1))
    grad_mlp = jnp.einsum("btf,df->btd", grad_up, up_full, preferred_element_type=f32)
    grad_scale_two = jnp.sum(grad_mlp * normed_two, axis=1)
    grad_shift_two = jnp.sum(grad_mlp, axis=1)
    grad_resid = grad_out + norm_back(grad_mlp * (1.0 + scale_two), normed_two, inverse_two)
    grad_gate_one = jnp.sum(grad_resid * attn_proj, axis=1)
    grad_proj = (grad_resid * gate_one).astype(bf16)
    gw_out = jnp.einsum("btd,bte->de", mixed_tokens, grad_proj, preferred_element_type=f32)
    own_out = reduce_rows(gw_out)
    gb_out = jnp.sum(grad_proj.astype(f32), axis=(0, 1))
    grad_mixed = jnp.einsum("bte,de->btd", grad_proj, out_full, preferred_element_type=f32).astype(
        bf16
    )
    grad_heads = grad_mixed.reshape(own_latents, tokens_all, H, HD).transpose(0, 2, 1, 3)
    grad_soft = jnp.einsum("bhqd,bhkd->bhqk", grad_heads, value_heads, preferred_element_type=f32)
    delta_sum = jnp.sum(soft_float * grad_soft, axis=-1, keepdims=True)
    grad_scores = (soft_float * (grad_soft - delta_sum)).astype(bf16)
    grad_queries = (
        jnp.einsum("bhqk,bhkd->bhqd", grad_scores, key_heads, preferred_element_type=f32)
        * scale_factor
    ).astype(bf16)
    grad_keys = (
        jnp.einsum("bhqk,bhqd->bhkd", grad_scores, queries, preferred_element_type=f32)
        * scale_factor
    ).astype(bf16)
    grad_values = jnp.einsum(
        "bhqk,bhqd->bhkd", soft_half, grad_heads, preferred_element_type=f32
    ).astype(bf16)
    grad_tokens = (
        jnp.stack([grad_queries, grad_keys, grad_values], axis=0)
        .transpose(1, 3, 0, 2, 4)
        .reshape(own_latents, tokens_all, 3 * D)
    )
    gw_qkv = jnp.einsum("btd,bte->de", attn_in, grad_tokens, preferred_element_type=f32)
    own_qkv = reduce_rows(gw_qkv)
    grad_tok_float = grad_tokens.astype(f32)
    gb_query = jnp.sum(grad_tok_float[:, :, :D], axis=(0, 1))
    gb_value = jnp.sum(grad_tok_float[:, :, 2 * D :], axis=(0, 1))
    grad_attn_in = jnp.einsum("bte,de->btd", grad_tokens, qkv_full, preferred_element_type=f32)
    grad_scale_one = jnp.sum(grad_attn_in * normed_one, axis=1)
    grad_shift_one = jnp.sum(grad_attn_in, axis=1)
    grad_latents = grad_resid + norm_back(grad_attn_in * (1.0 + scale_one), normed_one, inverse_one)
    grad_latents = lax.all_to_all(grad_latents, "sp", split_axis=1, concat_axis=0, tiled=True)
    grad_small = [
        grad_shift_one.reshape(-1),
        grad_scale_one.reshape(-1),
        grad_gate_one.reshape(-1),
        grad_shift_two.reshape(-1),
        grad_scale_two.reshape(-1),
        grad_gate_two.reshape(-1),
        gb_query,
        gb_value,
        gb_out,
        gb_up,
        gb_down,
    ]
    grad_small_all = lax.all_gather(jnp.concatenate(grad_small), ("fsdp", "sp"), axis=0)
    mod_width = 6 * own_latents * D
    grad_mod = (
        grad_small_all[:, :mod_width]
        .reshape(owners, 6, own_latents, D)
        .transpose(0, 2, 1, 3)
        .reshape(latent_total, 6 * D)
    )
    bias_sums = jnp.sum(grad_small_all[:, mod_width:], axis=0)
    own_bias = []
    start = 0
    for part in grad_small[6:]:
        piece = bias_sums[start : start + part.size].reshape(owners, -1)
        own_bias.append(lax.dynamic_index_in_dim(piece, owner_index, 0, False))
        start = start + part.size
    own_gb_query, own_gb_value, own_gb_out, own_gb_up, own_gb_down = own_bias
    silu_rows = lax.dynamic_index_in_dim(
        silu_all.reshape(latent_total, owners, D // owners), owner_index, 1, False
    )
    own_ada = jnp.dot(silu_rows.T, grad_mod, precision=lax.Precision.HIGHEST)
    own_gb_ada = lax.dynamic_index_in_dim(
        jnp.sum(grad_mod, axis=0).reshape(owners, -1), owner_index, 0, False
    )
    grad_silu = jnp.dot(grad_mod.astype(bf16), w_ada.T, preferred_element_type=f32)
    grad_silu = lax.all_to_all(
        grad_silu.reshape(fsdp_count, pair_latents * ada_rows),
        "fsdp",
        split_axis=0,
        concat_axis=0,
        tiled=True,
    )
    grad_silu = (
        grad_silu.reshape(fsdp_count, pair_latents, ada_rows)
        .transpose(1, 0, 2)
        .reshape(pair_latents, D)
    )
    grad_condition = silu_back(condition.astype(f32), grad_silu)
    return (
        output,
        grad_latents,
        grad_condition,
        own_ada,
        own_gb_ada,
        own_qkv,
        own_gb_query,
        own_gb_value,
        own_out,
        own_gb_out,
        own_up,
        own_gb_up,
        own_down,
        own_gb_down,
    )


def solution(mesh):
    in_specs = (
        P("fsdp", "sp", None),
        P("fsdp", None),
        P("fsdp", "sp", None),
        P("fsdp", None),
        P("fsdp"),
        P("fsdp", None),
        P("fsdp"),
        P("fsdp"),
        P("fsdp", None),
        P("fsdp"),
        P("fsdp", None),
        P("fsdp"),
        P("fsdp", None),
        P("fsdp"),
    )
    out_specs = (
        P("fsdp", "sp", None),
        P("fsdp", "sp", None),
        P("fsdp", None),
        P(("fsdp", "sp"), None),
        P(("fsdp", "sp")),
        P(("fsdp", "sp"), None),
        P(("fsdp", "sp")),
        P(("fsdp", "sp")),
        P(("fsdp", "sp"), None),
        P(("fsdp", "sp")),
        P(("fsdp", "sp"), None),
        P(("fsdp", "sp")),
        P(("fsdp", "sp"), None),
        P(("fsdp", "sp")),
    )
    return jax.shard_map(body, mesh=mesh, in_specs=in_specs, out_specs=out_specs, check_vma=False)
```

profile of v0, /device:TPU:0, one launch (start us, length us, event | category | flops | bytes accessed | tf_op | source)
XLA Modules:
  0.0 743.5 jit_solution(2040132775007080298)
XLA Ops:
  10.0 4.2 all-to-all-start
  14.9 4.1 concatenate.17
  19.1 22.7 %all_gather.21 = bf16[16,32,128]{2,1,0:T(8,128)(2,1)S(1)} all-gather(bf16[1,32,128]{2,1,0:T(8,128)(2,1)S(1)} %bitcast.185), channel_id=1, replica_groups=mesh['fsdp'=16,'sp'=2] {'fsdp'}, dimensions={0}, use_global_device_ids=true | all-gather | bytes 139264 | tf_op jit(solution)/shard_map/all_gather | solution.py:80
  43.7 3.5 all-to-all-start.1
  48.0 13.6 %all-to-all-done.1 = f32[16,1,4608]{2,1,0:T(1,128)S(1)} async-done(((f32[16,1,4608]{2,1,0:T(1,128)}), f32[16,1,4608]{2,1,0:T(1,128)S(1)}, u32[]{:S(2)}, u32[]{:S(2)}) %all-to-all-start.1) | async-done | bytes 294944 | tf_op jit(solution)/shard_map/all_to_all | solution.py:101
  61.7 3.8 all-to-all-start.3
  65.8 6.4 all-to-all-done.3
  73.4 4.2 fusion.1
  77.6 1.6 copy.62
  79.1 2.3 fusion.55
  81.4 4.8 convolution_convert_fusion.4
  86.2 18.5 %all-gather.10.cloned.1.call-done = bf16[768,768]{1,0:T(8,128)(2,1)} async-done(((bf16[48,768]{1,0:T(8,128)(2,1)}), bf16[768,768]{1,0:T(8,128)(2,1)}) %all-gather.10.cloned.1.call-update) | async-done | bytes 1179664 | tf_op jit(solution)/shard_map/all_gather | solution.py:113
  104.6 2.8 fusion.81
  107.7 51.3 %all-gather.14.cloned.1.call-done = bf16[3072,768]{1,0:T(8,128)(2,1)} async-done(((bf16[192,768]{1,0:T(8,128)(2,1)}), bf16[3072,768]{1,0:T(8,128)(2,1)}) %all-gather.14.cloned.1.call-update) | async-done | bytes 4718608 | tf_op jit(solution)/shard_map/all_gather | solution.py:115
  159.0 5.5 fusion.83
  164.5 48.3 %all-gather.12.cloned.1.call-done = bf16[768,3072]{1,0:T(8,128)(2,1)} async-done(((bf16[48,3072]{1,0:T(8,128)(2,1)}), bf16[768,3072]{1,0:T(8,128)(2,1)}) %all-gather.12.cloned.1.call-update) | async-done | bytes 4718608 | tf_op jit(solution)/shard_map/all_gather | solution.py:114
  212.8 7.0 convert_reduce_fusion
  219.9 1.8 multiply_reduce_fusion.1
  222.2 1.7 copy-done.3
  223.9 3.2 fusion.22
  229.3 4.8 fusion.17
  236.0 2.9 multiply_reduce_fusion
  242.0 1.5 convolution_convert_fusion.3
  243.5 1.4 pad_maximum_fusion
  244.9 4.2 fusion.36
  249.0 1.6 convert.10
  250.7 3.0 multiply_reduce_fusion.2
  255.1 2.9 convolution_convert_fusion.2
  258.1 1.3 copy-done.8
  259.5 3.7 convolution_convert_fusion.1
  264.1 6.3 convolution_convert_fusion
  272.6 3.0 reduce.57
  276.5 3.5 all-to-all-start.2
  279.9 1.7 copy.70
  281.6 5.5 all-to-all-done.2
  287.2 3.5 all-to-all-start.4
  292.4 11.1 %all-to-all-done.4 = f32[1,256,768]{2,0,1:T(1,128)S(1)} async-done(((f32[1,256,768]{2,0,1:T(1,128)}), f32[1,256,768]{2,0,1:T(1,128)S(1)}, u32[]{:S(2)}, u32[]{:S(2)}) %all-to-all-start.4) | async-done | bytes 786464 | tf_op jit(solution)/shard_map/all_to_all | solution.py:200
  304.4 42.0 %reduce-scatter.7.cloned.1.call-done = bf16[24,768]{1,0:T(8,128)(2,1)} async-done(((bf16[768,768]{1,0:T(8,128)(2,1)}), bf16[24,768]{1,0:T(8,128)(2,1)}) %reduce-scatter.7.cloned.1.call-update) | async-done | bytes 36880 | tf_op jit(solution)/shard_map/reduce_scatter | solution.py:42
  346.3 1.4 convert_element_type.318
  347.7 55.6 %all-gather.16.cloned.1.call-done = f32[32,1,10752]{2,1,0:T(1,128)} async-done(((f32[1,1,10752]{2,1,0:T(1,128)}), f32[32,1,10752]{2,1,0:T(1,128)}) %all-gather.16.cloned.1.call-update) | async-done | bytes 1376272 | tf_op jit(solution)/shard_map/all_gather | solution.py:214
  403.3 1.4 copy.91
  405.7 4.6 all-to-all-start.5
  418.6 92.5 %reduce-scatter.5.cloned.1.call-done = bf16[24,2304]{1,0:T(8,128)(2,1)} async-done(((bf16[768,2304]{1,0:T(8,128)(2,1)}), bf16[24,2304]{1,0:T(8,128)(2,1)}) %reduce-scatter.5.cloned.1.call-update) | async-done | bytes 110608 | tf_op jit(solution)/shard_map/reduce_scatter | solution.py:42
  511.1 1.6 convert_element_type.316
  512.7 110.3 %reduce-scatter.9.cloned.1.call-done = bf16[24,3072]{1,0:T(8,128)(2,1)} async-done(((bf16[768,3072]{1,0:T(8,128)(2,1)}), bf16[24,3072]{1,0:T(8,128)(2,1)}) %reduce-scatter.9.cloned.1.call-update) | async-done | bytes 147472 | tf_op jit(solution)/shard_map/reduce_scatter | solution.py:42
  623.0 1.6 convert_element_type.320
  624.6 110.7 %reduce-scatter.11.cloned.1.call-done = bf16[96,768]{1,0:T(8,128)(2,1)} async-done(((bf16[3072,768]{1,0:T(8,128)(2,1)}), bf16[96,768]{1,0:T(8,128)(2,1)}) %reduce-scatter.11.cloned.1.call-update) | async-done | bytes 147472 | tf_op jit(solution)/shard_map/reduce_scatter | solution.py:42
  735.3 1.6 convert_element_type.322
  (147 shorter events, 32.5 us)
Async XLA Ops:
  7.2 35.0 %copy-start = (bf16[48,4608]{1,0:T(8,128)(2,1)S(1)}, bf16[48,4608]{1,0:T(8,128)(2,1)}, u32[]{:S(2)}) copy-start(bf16[48,4608]{1,0:T(8,128)(2,1)} %param.17) | copy-start | bytes 1327108
  7.2 66.2 %all-gather.8.cloned.1.call-start = ((), (), s32[]{:S(2)}) async-start(), calls=%async_computation.10 | async-start | bytes 3760128 | tf_op jit(solution)/shard_map/all_gather | solution.py:112
  7.9 96.7 %all-gather.10.cloned.1.call-start = ((), (), s32[]{:S(2)}) async-start(), calls=%async_computation.11 | async-start | bytes 1253376 | tf_op jit(solution)/shard_map/all_gather | solution.py:113
  8.7 150.3 %all-gather.14.cloned.1.call-start = ((), (), s32[]{:S(2)}) async-start(), calls=%async_computation.13 | async-start | bytes 5013504 | tf_op jit(solution)/shard_map/all_gather | solution.py:115
  9.4 203.4 %all-gather.12.cloned.1.call-start = ((), (), s32[]{:S(2)}) async-start(), calls=%async_computation.12 | async-start | bytes 5013504 | tf_op jit(solution)/shard_map/all_gather | solution.py:114
  10.0 33.7 %all-to-all-start = ((bf16[2,128,768]{2,1,0:T(8,128)(2,1)}), bf16[2,128,768]{2,1,0:T(8,128)(2,1)S(1)}, u32[]{:S(2)}, u32[]{:S(2)}) async-start(bf16[2,128,768]{2,1,0:T(8,128)(2,1)} %param.14), calls=%async_computation | async-start | bytes 786432 | tf_op jit(solution)/shard_map/all_to_all | solution.py:91
  43.7 17.9 %all-to-all-start.1 = ((f32[16,1,4608]{2,1,0:T(1,128)}), f32[16,1,4608]{2,1,0:T(1,128)S(1)}, u32[]{:S(2)}, u32[]{:S(2)}) async-start(f32[16,1,4608]{2,1,0:T(1,128)} %copy.61), calls=%async_computation.1 | async-start | bytes 589824 | tf_op jit(solution)/shard_map/all_to_all | solution.py:101
  61.7 10.5 %all-to-all-start.3 = ((bf16[2,128,768]{2,1,0:T(8,128)(2,1)}), bf16[2,128,768]{2,1,0:T(8,128)(2,1)S(1)}, u32[]{:S(2)}, u32[]{:S(2)}) async-start(bf16[2,128,768]{2,1,0:T(8,128)(2,1)} %param.16), calls=%async_computation.3 | async-start | bytes 786432 | tf_op jit(solution)/shard_map/all_to_all | solution.py:92
  65.5 280.9 %reduce-scatter.7.cloned.1.call-start = ((), (), s32[]{:S(2)}) async-start(), calls=%async_computation.15 | async-start | bytes 1216512 | tf_op jit(solution)/shard_map/reduce_scatter | solution.py:42
  212.8 7.1 copy-start.15
  219.8 1.8 copy-start.7
  219.8 2.4 copy-start.16
  219.9 4.0 copy-start.3
  223.9 3.9 copy-start.4
  227.1 0.7 copy-start.10
  229.3 4.8 copy-start.12
  234.1 1.9 copy-start.1
  239.5 2.5 copy-start.9
  239.5 2.5 copy-start.11
  250.7 152.7 %all-gather.16.cloned.1.call-start = ((), (), s32[]{:S(2)}) async-start(), calls=%async_computation.18 | async-start | bytes 1419264 | tf_op jit(solution)/shard_map/all_gather | solution.py:214
  250.7 3.1 copy-start.2
  254.8 256.3 %reduce-scatter.5.cloned.1.call-start = ((), (), s32[]{:S(2)}) async-start(), calls=%async_computation.14 | async-start | bytes 3649536 | tf_op jit(solution)/shard_map/reduce_scatter | solution.py:42
  258.0 1.4 copy-start.8
  258.1 364.9 %reduce-scatter.9.cloned.1.call-start = ((), (), s32[]{:S(2)}) async-start(), calls=%async_computation.16 | async-start | bytes 4866048 | tf_op jit(solution)/shard_map/reduce_scatter | solution.py:42
  263.2 1.0 copy-start.6
  263.2 472.2 %reduce-scatter.11.cloned.1.call-start = ((), (), s32[]{:S(2)}) async-start(), calls=%async_computation.17 | async-start | bytes 4866048 | tf_op jit(solution)/shard_map/reduce_scatter | solution.py:42
  270.5 1.0 copy-start.13
  270.5 9.4 %copy-start.5 = (f32[256,768]{1,0:T(8,128)S(1)}, f32[256,768]{1,0:T(8,128)}, u32[]{:S(2)}) copy-start(f32[256,768]{1,0:T(8,128)} %get-tuple-element.43) | copy-start | bytes 2359300
  276.5 10.7 %all-to-all-start.2 = ((bf16[2,2,49152]{2,1,0:T(2,128)(2,1)}), bf16[2,2,49152]{2,1,0:T(2,128)(2,1)S(1)}, u32[]{:S(2)}, u32[]{:S(2)}) async-start(bf16[2,2,49152]{2,1,0:T(2,128)(2,1)} %reshape.788), calls=%async_computation.2 | async-start | bytes 786432 | tf_op jit(solution)/shard_map/all_to_all | solution.py:148
  287.2 16.3 %all-to-all-start.4 = ((f32[1,256,768]{2,0,1:T(1,128)}), f32[1,256,768]{2,0,1:T(1,128)S(1)}, u32[]{:S(2)}, u32[]{:S(2)}) async-start(f32[1,256,768]{2,0,1:T(1,128)} %copy.70), calls=%async_computation.4 | async-start | bytes 1572864 | tf_op jit(solution)/shard_map/all_to_all | solution.py:200
  347.7 70.2 %copy-start.14 = (bf16[2,768]{1,0:T(2,128)(2,1)S(1)}, bf16[2,768]{1,0:T(2,128)(2,1)}, u32[]{:S(2)}) copy-start(bf16[2,768]{1,0:T(2,128)(2,1)} %param.15) | copy-start | bytes 9220
  405.7 11.0 %all-to-all-start.5 = ((f32[16,1,96]{2,1,0:T(1,128)}), f32[16,1,96]{2,1,0:T(1,128)S(1)}, u32[]{:S(2)}, u32[]{:S(2)}) async-start(f32[16,1,96]{2,1,0:T(1,128)} %bitcast.31), calls=%async_computation.5 | async-start | bytes 16384 | tf_op jit(solution)/shard_map/all_to_all | solution.py:238
Sparse Core Ops, SparseCore 0:
  10.3 55.0 all-gather.7
  67.7 36.8 all-gather.9
  106.9 51.9 all-gather.13
  161.1 51.6 all-gather.11
  250.8 95.5 reduce-scatter.6
  349.6 53.6 all-gather.15
  408.7 102.3 reduce-scatter.4
  516.6 106.3 reduce-scatter.8
  628.5 106.8 reduce-scatter.10
where the time goes:
time: 745 us; the launch traced here: 744 us
  waiting for transfers between devices  570 us (77%)
  matrix products  60.4 us (8%)
  local copies, waits for them, and re-layouts  29.6 us (4%)
  starting transfers between devices  23.8 us (3%)
  other arithmetic  23 us (3%)
  blocking collectives  22.7 us (3%)
  between operations  14.4 us (2%)
    reduce_scatter x4, waiting for transfers between devices, reduce_rows(): lax.psum_scatter(grad.astype(jnp.bfloat16), ('fsdp', 'sp'), scatter_dimen...  355 us
    all_gather x1, waiting for transfers between devices, body(): lax.all_gather(jnp.concatenate(grad_small), ('fsdp', 'sp'), axis=0)  55.6 us
    all_gather x1, waiting for transfers between devices, body(): down_full = lax.all_gather(w_down, 'fsdp', axis=0, tiled=True)  51.3 us
    all_gather x1, waiting for transfers between devices, body(): up_full = lax.all_gather(w_up, 'fsdp', axis=0, tiled=True)  48.3 us
    all_gather x1, blocking collectives, body(): lax.all_gather(jnp.concatenate(small).reshape(1, padded // 128, 128), 'fs...  22.7 us
    all_gather x1, waiting for transfers between devices, body(): out_full = lax.all_gather(w_out, 'fsdp', axis=0, tiled=True)  18.5 us
  transfers between devices with their start and end apart: 15, of which 13 were waited for; matrix products, arithmetic and copies ran while one was open for 9% of the time, Pallas kernels for 0%

commit v1 on v0

--- a/solution.py
+++ b/solution.py
@@ -2,6 +2,7 @@
 import jax.numpy as jnp
 from jax import lax
 from jax.sharding import PartitionSpec as P
+from jax.lax import axis_index, axis_size, ppermute
 
 D = 768
 H = 12
@@ -112,7 +113,25 @@
     qkv_full = lax.all_gather(w_qkv, "fsdp", axis=0, tiled=True)
     out_full = lax.all_gather(w_out, "fsdp", axis=0, tiled=True)
     up_full = lax.all_gather(w_up, "fsdp", axis=0, tiled=True)
-    down_full = lax.all_gather(w_down, "fsdp", axis=0, tiled=True)
+    inter = axis_index("fsdp")
+    piece_now = axis_size("fsdp")
+    w1, mat_out, z_new = (piece_now, inter, w_down.shape[0])
+    panels = [(k0, (k0 + 1) % w1) for k0 in range(w1)]
+    down_full = jnp.zeros((*w_down.shape[:0], w1 * z_new, *w_down.shape[1:]), w_down.dtype)
+    parts_seen = [(k0, (k0 - 1) % w1) for k0 in range(w1)]
+    piece_next = everything = w_down
+    f_now = w1 // 2
+    down_full = lax.dynamic_update_slice_in_dim(down_full, w_down, mat_out * z_new, axis=0)
+    for src_i in range(1, f_now + 1):
+        piece_next = ppermute(piece_next, axis_name="fsdp", perm=panels)
+        down_full = lax.dynamic_update_slice_in_dim(
+            down_full, piece_next, (mat_out - src_i) % w1 * z_new, axis=0
+        )
+        if src_i < w1 - f_now:
+            everything = ppermute(everything, axis_name="fsdp", perm=parts_seen)
+            down_full = lax.dynamic_update_slice_in_dim(
+                down_full, everything, (mat_out + src_i) % w1 * z_new, axis=0
+            )
     normed_one, inverse_one = normalize(inputs)
     attn_in = (normed_one * (1.0 + scale_one) + shift_one).astype(bf16)
     qkv_bias = jnp.concatenate([query_bias, jnp.zeros_like(query_bias), value_bias]).astype(f32)

time: 745 us -> 700 us (0.940)
  waiting for transfers between devices: 570 us -> 481 us
  starting transfers between devices: 23.8 us -> 56.4 us
  local copies, waits for them, and re-layouts: 29.6 us -> 42.9 us
    all_gather x1 -> x0, waiting for transfers between devices: 51.3 us -> none  [body(): down_full = lax.all_gather(w_down, 'fsdp', axis=0, tiled=True)]
    ppermute x0 -> x15, starting transfers between devices: none -> 33.8 us  [the longest x7 32.8 us: body(): everything = ppermute(everything, axis_name='fsdp', perm=parts_seen)]
    all_gather x1, waiting for transfers between devices: 48.3 us -> 15.4 us  [body(): up_full = lax.all_gather(w_up, 'fsdp', axis=0, tiled=True)]
    ppermute x0 -> x15, waiting for transfers between devices: none -> 29 us  [the longest x8 24.8 us: body(): piece_next = ppermute(piece_next, axis_name='fsdp', perm=panels)]
    all_gather x1, waiting for transfers between devices: 18.5 us -> 0.01 us  [body(): out_full = lax.all_gather(w_out, 'fsdp', axis=0, tiled=True)]
    dynamic_update_slice x0 -> x16, local copies, waits for them, and re-layouts: none -> 12.8 us  [the longest x8 6.97 us: body(): lax.dynamic_update_slice_in_dim(down_full, piece_next, (mat_out - src_i)...]
    all_to_all x1, waiting for transfers between devices: 13.6 us -> 5.92 us  [body(): lax.all_to_all(mod_part.reshape(fsdp_count, own_latents * 6 * D), 'fsdp',...]
  transfers between devices with their start and end apart: 15 -> 29, of which waited for: 13 -> 18; matrix products, arithmetic and copies ran while one was open for 9% -> 11% of each run, Pallas kernels for 0% -> 0%
where the time goes in v1:
time: 700 us; the launch traced here: 699 us
  waiting for transfers between devices  481 us (69%)
  matrix products  60.4 us (9%)
  starting transfers between devices  56.4 us (8%)
  local copies, waits for them, and re-layouts  42.9 us (6%)
  other arithmetic  23 us (3%)
  blocking collectives  19.9 us (3%)
  between operations  15.1 us (2%)
    reduce_scatter x4, waiting for transfers between devices, reduce_rows(): lax.psum_scatter(grad.astype(jnp.bfloat16), ('fsdp', 'sp'), scatter_dimen...  355 us
    all_gather x1, waiting for transfers between devices, body(): lax.all_gather(jnp.concatenate(grad_small), ('fsdp', 'sp'), axis=0)  55.5 us
    ppermute x7, starting transfers between devices, body(): everything = ppermute(everything, axis_name='fsdp', perm=parts_seen)  32.8 us
    ppermute x8, waiting for transfers between devices, body(): piece_next = ppermute(piece_next, axis_name='fsdp', perm=panels)  24.8 us
    all_gather x1, blocking collectives, body(): lax.all_gather(jnp.concatenate(small).reshape(1, padded // 128, 128), 'fs...  19.9 us
    all_gather x1, waiting for transfers between devices, body(): up_full = lax.all_gather(w_up, 'fsdp', axis=0, tiled=True)  15.4 us
  transfers between devices with their start and end apart: 29, of which 18 were waited for; matrix products, arithmetic and copies ran while one was open for 11% of the time, Pallas kernels for 0%

profile of v1, /device:TPU:0, one launch (start us, length us, event | category | flops | bytes accessed | tf_op | source)
XLA Modules:
  0.0 699.0 jit_solution(17748478819968856416)
XLA Ops:
  10.0 5.0 collective-permute-start.1
  15.0 3.5 all-to-all-start
  19.5 4.1 concatenate.17
  23.6 19.9 %all_gather.18 = bf16[16,32,128]{2,1,0:T(8,128)(2,1)S(1)} all-gather(bf16[1,32,128]{2,1,0:T(8,128)(2,1)S(1)} %bitcast.185), channel_id=1, replica_groups=mesh['fsdp'=16,'sp'=2] {'fsdp'}, dimensions={0}, use_global_device_ids=true | all-gather | bytes 139264 | tf_op jit(solution)/shard_map/all_gather | solution.py:81
  45.8 2.5 broadcast_in_dim.8
  49.0 3.5 all-to-all-start.1
  53.3 4.2 collective-permute-start.3
  59.0 5.9 all-to-all-done.1
  64.9 3.5 all-to-all-start.3
  68.8 5.6 collective-permute-start.5
  74.7 4.5 collective-permute-done.4
  80.1 4.4 collective-permute-start.7
  84.6 3.9 collective-permute-done.6
  90.0 4.5 collective-permute-start.9
  95.3 4.5 collective-permute-done.8
  100.5 1.7 constant_dynamic-update-slice_fusion.8
  102.3 4.4 collective-permute-start.11
  110.9 4.7 collective-permute-start.13
  116.3 1.7 collective-permute-done.12
  119.6 3.9 collective-permute-done.13
  124.2 8.3 %collective-permute-done.14 = bf16[192,768]{1,0:T(8,128)(2,1)S(1)} collective-permute-done((bf16[192,768]{1,0:T(8,128)(2,1)S(1)}, bf16[192,768]{1,0:T(8,128)(2,1)S(1)}, u32[]{:S(2)}, u32[]{:S(2)}) %collective-permute-start.14) | collective-permute-done | bytes 294944 | tf_op jit(solution)/shard_map/ppermute | solution.py:126
  133.3 4.1 fusion.1
  137.4 1.7 copy.62
  139.1 2.3 fusion.55
  141.5 4.8 convolution_convert_fusion.4
  146.2 2.8 fusion.81
  149.3 15.4 %all-gather.11.cloned.1.call-done = bf16[768,3072]{1,0:T(8,128)(2,1)} async-done(((bf16[48,3072]{1,0:T(8,128)(2,1)}), bf16[768,3072]{1,0:T(8,128)(2,1)}) %all-gather.11.cloned.1.call-update) | async-done | bytes 4718608 | tf_op jit(solution)/shard_map/all_gather | solution.py:115
  164.7 4.0 convolution_add_fusion.1
  168.7 6.4 convert_reduce_fusion
  176.8 5.6 fusion.22
  184.6 4.8 fusion.17
  191.4 2.9 multiply_reduce_fusion
  200.3 4.2 fusion.36
  206.2 3.0 multiply_reduce_fusion.2
  210.5 2.9 convolution_convert_fusion.2
  214.9 3.7 convolution_convert_fusion.1
  219.5 6.3 convolution_convert_fusion
  228.0 3.0 reduce.57
  231.9 3.5 all-to-all-start.2
  237.0 5.5 all-to-all-done.2
  242.6 3.5 all-to-all-start.4
  247.7 11.1 %all-to-all-done.4 = f32[1,256,768]{2,0,1:T(1,128)S(1)} async-done(((f32[1,256,768]{2,0,1:T(1,128)}), f32[1,256,768]{2,0,1:T(1,128)S(1)}, u32[]{:S(2)}, u32[]{:S(2)}) %all-to-all-start.4) | async-done | bytes 786464 | tf_op jit(solution)/shard_map/all_to_all | solution.py:219
  259.8 42.1 %reduce-scatter.7.cloned.1.call-done = bf16[24,768]{1,0:T(8,128)(2,1)} async-done(((bf16[768,768]{1,0:T(8,128)(2,1)}), bf16[24,768]{1,0:T(8,128)(2,1)}) %reduce-scatter.7.cloned.1.call-update) | async-done | bytes 36880 | tf_op jit(solution)/shard_map/reduce_scatter | solution.py:43
  303.2 55.5 %all-gather.13.cloned.1.call-done = f32[32,1,10752]{2,1,0:T(1,128)} async-done(((f32[1,1,10752]{2,1,0:T(1,128)}), f32[32,1,10752]{2,1,0:T(1,128)}) %all-gather.13.cloned.1.call-update) | async-done | bytes 1376272 | tf_op jit(solution)/shard_map/all_gather | solution.py:233
  361.1 4.6 all-to-all-start.5
  374.1 92.3 %reduce-scatter.5.cloned.1.call-done = bf16[24,2304]{1,0:T(8,128)(2,1)} async-done(((bf16[768,2304]{1,0:T(8,128)(2,1)}), bf16[24,2304]{1,0:T(8,128)(2,1)}) %reduce-scatter.5.cloned.1.call-update) | async-done | bytes 110608 | tf_op jit(solution)/shard_map/reduce_scatter | solution.py:43
  468.0 110.5 %reduce-scatter.9.cloned.1.call-done = bf16[24,3072]{1,0:T(8,128)(2,1)} async-done(((bf16[768,3072]{1,0:T(8,128)(2,1)}), bf16[24,3072]{1,0:T(8,128)(2,1)}) %reduce-scatter.9.cloned.1.call-update) | async-done | bytes 147472 | tf_op jit(solution)/shard_map/reduce_scatter | solution.py:43
  580.1 110.3 %reduce-scatter.11.cloned.1.call-done = bf16[96,768]{1,0:T(8,128)(2,1)} async-done(((bf16[3072,768]{1,0:T(8,128)(2,1)}), bf16[96,768]{1,0:T(8,128)(2,1)}) %reduce-scatter.11.cloned.1.call-update) | async-done | bytes 147472 | tf_op jit(solution)/shard_map/reduce_scatter | solution.py:43
  (196 shorter events, 62.5 us)
Async XLA Ops:
  7.2 36.7 %copy-start = (bf16[48,4608]{1,0:T(8,128)(2,1)S(1)}, bf16[48,4608]{1,0:T(8,128)(2,1)}, u32[]{:S(2)}) copy-start(bf16[48,4608]{1,0:T(8,128)(2,1)} %param.17) | copy-start | bytes 1327108
  7.2 126.1 %all-gather.7.cloned.1.call-start = ((), (), s32[]{:S(2)}) async-start(), calls=%async_computation.10 | async-start | bytes 3760128 | tf_op jit(solution)/shard_map/all_gather | solution.py:113
  7.9 138.3 %all-gather.9.cloned.1.call-start = ((), (), s32[]{:S(2)}) async-start(), calls=%async_computation.11 | async-start | bytes 1253376 | tf_op jit(solution)/shard_map/all_gather | solution.py:114
  8.7 156.0 %all-gather.11.cloned.1.call-start = ((), (), s32[]{:S(2)}) async-start(), calls=%async_computation.12 | async-start | bytes 5013504 | tf_op jit(solution)/shard_map/all_gather | solution.py:115
  9.4 43.6 %collective-permute-start = (bf16[192,768]{1,0:T(8,128)(2,1)}, bf16[192,768]{1,0:T(8,128)(2,1)S(1)}, u32[]{:S(2)}, u32[]{:S(2)}) collective-permute-start(bf16[192,768]{1,0:T(8,128)(2,1)} %param.26), channel_id=1, source_target_pairs={{0,2},{2,4},{4,6},{6,8},{8,10},{10,12},{12,14},{14,16},{16,18},{18... | collective-permute-start | bytes 884744 | tf_op jit(solution)/shard_map/ppermute | solution.py:126
  10.0 43.4 %collective-permute-start.1 = (bf16[192,768]{1,0:T(8,128)(2,1)}, bf16[192,768]{1,0:T(8,128)(2,1)S(1)}, u32[]{:S(2)}, u32[]{:S(2)}) collective-permute-start(bf16[192,768]{1,0:T(8,128)(2,1)} %param.26), channel_id=1, source_target_pairs={{0,30},{2,0},{4,2},{6,4},{8,6},{10,8},{12,10},{14,12},{16,14},{18,... | collective-permute-start | bytes 884744 | tf_op jit(solution)/shard_map/ppermute | solution.py:131
  15.0 34.0 %all-to-all-start = ((bf16[2,128,768]{2,1,0:T(8,128)(2,1)}), bf16[2,128,768]{2,1,0:T(8,128)(2,1)S(1)}, u32[]{:S(2)}, u32[]{:S(2)}) async-start(bf16[2,128,768]{2,1,0:T(8,128)(2,1)} %param.14), calls=%async_computation | async-start | bytes 786432 | tf_op jit(solution)/shard_map/all_to_all | solution.py:92
  43.9 4.4 copy-start.14
  49.0 15.9 %all-to-all-start.1 = ((f32[16,1,4608]{2,1,0:T(1,128)}), f32[16,1,4608]{2,1,0:T(1,128)S(1)}, u32[]{:S(2)}, u32[]{:S(2)}) async-start(f32[16,1,4608]{2,1,0:T(1,128)} %copy.61), calls=%async_computation.1 | async-start | bytes 589824 | tf_op jit(solution)/shard_map/all_to_all | solution.py:102
  53.0 15.7 %collective-permute-start.2 = (bf16[192,768]{1,0:T(8,128)(2,1)S(1)}, bf16[192,768]{1,0:T(8,128)(2,1)S(1)}, u32[]{:S(2)}, u32[]{:S(2)}) collective-permute-start(bf16[192,768]{1,0:T(8,128)(2,1)S(1)} %collective-permute-done), channel_id=1, source_target_pairs={{0,2},{2,4},{4,6},{6,8},{8,10},{10,12},{12,14},{14,16},{16,18},{18... | collective-permute-start | bytes 884744 | tf_op jit(solution)/shard_map/ppermute | solution.py:126
  53.3 15.5 %collective-permute-start.3 = (bf16[192,768]{1,0:T(8,128)(2,1)S(1)}, bf16[192,768]{1,0:T(8,128)(2,1)S(1)}, u32[]{:S(2)}, u32[]{:S(2)}) collective-permute-start(bf16[192,768]{1,0:T(8,128)(2,1)S(1)} %collective-permute-done.1), channel_id=1, source_target_pairs={{0,30},{2,0},{4,2},{6,4},{8,6},{10,8},{12,10},{14,12},{16,14},{18,... | collective-permute-start | bytes 884744 | tf_op jit(solution)/shard_map/ppermute | solution.py:131
  64.9 14.3 %all-to-all-start.3 = ((bf16[2,128,768]{2,1,0:T(8,128)(2,1)}), bf16[2,128,768]{2,1,0:T(8,128)(2,1)S(1)}, u32[]{:S(2)}, u32[]{:S(2)}) async-start(bf16[2,128,768]{2,1,0:T(8,128)(2,1)} %param.16), calls=%async_computation.3 | async-start | bytes 786432 | tf_op jit(solution)/shard_map/all_to_all | solution.py:93
  68.4 233.4 %reduce-scatter.7.cloned.1.call-start = ((), (), s32[]{:S(2)}) async-start(), calls=%async_computation.14 | async-start | bytes 1216512 | tf_op jit(solution)/shard_map/reduce_scatter | solution.py:43
  68.7 10.5 %collective-permute-start.4 = (bf16[192,768]{1,0:T(8,128)(2,1)S(1)}, bf16[192,768]{1,0:T(8,128)(2,1)S(1)}, u32[]{:S(2)}, u32[]{:S(2)}) collective-permute-start(bf16[192,768]{1,0:T(8,128)(2,1)S(1)} %collective-permute-done.2), channel_id=1, source_target_pairs={{0,2},{2,4},{4,6},{6,8},{8,10},{10,12},{12,14},{14,16},{16,18},{18... | collective-permute-start | bytes 884744 | tf_op jit(solution)/shard_map/ppermute | solution.py:126
  68.8 11.2 %collective-permute-start.5 = (bf16[192,768]{1,0:T(8,128)(2,1)S(1)}, bf16[192,768]{1,0:T(8,128)(2,1)S(1)}, u32[]{:S(2)}, u32[]{:S(2)}) collective-permute-start(bf16[192,768]{1,0:T(8,128)(2,1)S(1)} %collective-permute-done.3), channel_id=1, source_target_pairs={{0,30},{2,0},{4,2},{6,4},{8,6},{10,8},{12,10},{14,12},{16,14},{18,... | collective-permute-start | bytes 884744 | tf_op jit(solution)/shard_map/ppermute | solution.py:131
  79.2 9.3 %collective-permute-start.6 = (bf16[192,768]{1,0:T(8,128)(2,1)S(1)}, bf16[192,768]{1,0:T(8,128)(2,1)}, u32[]{:S(2)}, u32[]{:S(2)}) collective-permute-start(bf16[192,768]{1,0:T(8,128)(2,1)S(1)} %collective-permute-done.4), channel_id=1, source_target_pairs={{0,2},{2,4},{4,6},{6,8},{8,10},{10,12},{12,14},{14,16},{16,18},{18... | collective-permute-start | bytes 884744 | tf_op jit(solution)/shard_map/ppermute | solution.py:126
  80.1 10.0 %collective-permute-start.7 = (bf16[192,768]{1,0:T(8,128)(2,1)S(1)}, bf16[192,768]{1,0:T(8,128)(2,1)S(1)}, u32[]{:S(2)}, u32[]{:S(2)}) collective-permute-start(bf16[192,768]{1,0:T(8,128)(2,1)S(1)} %collective-permute-done.5), channel_id=1, source_target_pairs={{0,30},{2,0},{4,2},{6,4},{8,6},{10,8},{12,10},{14,12},{16,14},{18,... | collective-permute-start | bytes 884744 | tf_op jit(solution)/shard_map/ppermute | solution.py:131
  88.5 11.3 %collective-permute-start.8 = (bf16[192,768]{1,0:T(8,128)(2,1)}, bf16[192,768]{1,0:T(8,128)(2,1)S(1)}, u32[]{:S(2)}, u32[]{:S(2)}) collective-permute-start(bf16[192,768]{1,0:T(8,128)(2,1)} %collective-permute-done.6), channel_id=1, source_target_pairs={{0,2},{2,4},{4,6},{6,8},{8,10},{10,12},{12,14},{14,16},{16,18},{18... | collective-permute-start | bytes 884744 | tf_op jit(solution)/shard_map/ppermute | solution.py:126
  90.0 12.3 %collective-permute-start.9 = (bf16[192,768]{1,0:T(8,128)(2,1)S(1)}, bf16[192,768]{1,0:T(8,128)(2,1)S(1)}, u32[]{:S(2)}, u32[]{:S(2)}) collective-permute-start(bf16[192,768]{1,0:T(8,128)(2,1)S(1)} %collective-permute-done.7), channel_id=1, source_target_pairs={{0,30},{2,0},{4,2},{6,4},{8,6},{10,8},{12,10},{14,12},{16,14},{18,... | collective-permute-start | bytes 884744 | tf_op jit(solution)/shard_map/ppermute | solution.py:131
  99.8 9.3 %collective-permute-start.10 = (bf16[192,768]{1,0:T(8,128)(2,1)S(1)}, bf16[192,768]{1,0:T(8,128)(2,1)S(1)}, u32[]{:S(2)}, u32[]{:S(2)}) collective-permute-start(bf16[192,768]{1,0:T(8,128)(2,1)S(1)} %collective-permute-done.8), channel_id=1, source_target_pairs={{0,2},{2,4},{4,6},{6,8},{8,10},{10,12},{12,14},{14,16},{16,18},{18... | collective-permute-start | bytes 884744 | tf_op jit(solution)/shard_map/ppermute | solution.py:126
  102.3 8.6 %collective-permute-start.11 = (bf16[192,768]{1,0:T(8,128)(2,1)S(1)}, bf16[192,768]{1,0:T(8,128)(2,1)S(1)}, u32[]{:S(2)}, u32[]{:S(2)}) collective-permute-start(bf16[192,768]{1,0:T(8,128)(2,1)S(1)} %collective-permute-done.9), channel_id=1, source_target_pairs={{0,30},{2,0},{4,2},{6,4},{8,6},{10,8},{12,10},{14,12},{16,14},{18,... | collective-permute-start | bytes 884744 | tf_op jit(solution)/shard_map/ppermute | solution.py:131
  109.1 8.9 %collective-permute-start.12 = (bf16[192,768]{1,0:T(8,128)(2,1)S(1)}, bf16[192,768]{1,0:T(8,128)(2,1)S(1)}, u32[]{:S(2)}, u32[]{:S(2)}) collective-permute-start(bf16[192,768]{1,0:T(8,128)(2,1)S(1)} %collective-permute-done.10), channel_id=1, source_target_pairs={{0,2},{2,4},{4,6},{6,8},{8,10},{10,12},{12,14},{14,16},{16,18},{18... | collective-permute-start | bytes 884744 | tf_op jit(solution)/shard_map/ppermute | solution.py:126
  110.9 12.5 %collective-permute-start.13 = (bf16[192,768]{1,0:T(8,128)(2,1)S(1)}, bf16[192,768]{1,0:T(8,128)(2,1)S(1)}, u32[]{:S(2)}, u32[]{:S(2)}) collective-permute-start(bf16[192,768]{1,0:T(8,128)(2,1)S(1)} %collective-permute-done.11), channel_id=1, source_target_pairs={{0,30},{2,0},{4,2},{6,4},{8,6},{10,8},{12,10},{14,12},{16,14},{18,... | collective-permute-start | bytes 884744 | tf_op jit(solution)/shard_map/ppermute | solution.py:131
  118.1 14.4 %collective-permute-start.14 = (bf16[192,768]{1,0:T(8,128)(2,1)S(1)}, bf16[192,768]{1,0:T(8,128)(2,1)S(1)}, u32[]{:S(2)}, u32[]{:S(2)}) collective-permute-start(bf16[192,768]{1,0:T(8,128)(2,1)S(1)} %collective-permute-done.12), channel_id=1, source_target_pairs={{0,2},{2,4},{4,6},{6,8},{8,10},{10,12},{12,14},{14,16},{16,18},{18... | collective-permute-start | bytes 884744 | tf_op jit(solution)/shard_map/ppermute | solution.py:126
  164.7 4.0 copy-start.11
  164.7 10.4 %slice-start = ((s8[4718592]{0:T(1024)(128)(4,1)}), s8[4194304]{0:T(1024)(128)(4,1)S(1)}, s32[]{:S(2)}) async-start(s8[4718592]{0:T(1024)(128)(4,1)} %bitcast.187), calls=%async_computation.18 | async-start | bytes 8388608
  168.7 8.1 %copy-start.16 = (f32[256,3072]{1,0:T(8,128)}, f32[256,3072]{1,0:T(8,128)S(1)}, u32[]{:S(2)}) copy-start(f32[256,3072]{1,0:T(8,128)S(1)} %convolution_add_fusion.1) | copy-start | bytes 9437188
  168.7 6.4 slice-start.1
  175.1 1.7 copy-start.5
  176.8 6.4 copy-start.3
  182.4 0.8 copy-start.8
  184.6 4.8 copy-start.10
  189.5 1.9 copy-start.1
  194.8 2.6 copy-start.7
  194.9 2.5 copy-start.9
  206.1 152.7 %all-gather.13.cloned.1.call-start = ((), (), s32[]{:S(2)}) async-start(), calls=%async_computation.17 | async-start | bytes 1419264 | tf_op jit(solution)/shard_map/all_gather | solution.py:233
  206.1 3.1 copy-start.2
  210.2 256.2 %reduce-scatter.5.cloned.1.call-start = ((), (), s32[]{:S(2)}) async-start(), calls=%async_computation.13 | async-start | bytes 3649536 | tf_op jit(solution)/shard_map/reduce_scatter | solution.py:43
  213.4 1.4 copy-start.6
  213.5 365.0 %reduce-scatter.9.cloned.1.call-start = ((), (), s32[]{:S(2)}) async-start(), calls=%async_computation.15 | async-start | bytes 4866048 | tf_op jit(solution)/shard_map/reduce_scatter | solution.py:43
  218.6 1.0 copy-start.12
  218.6 471.9 %reduce-scatter.11.cloned.1.call-start = ((), (), s32[]{:S(2)}) async-start(), calls=%async_computation.16 | async-start | bytes 4866048 | tf_op jit(solution)/shard_map/reduce_scatter | solution.py:43
  225.9 1.0 copy-start.13
  225.9 9.4 %copy-start.4 = (f32[256,768]{1,0:T(8,128)S(1)}, f32[256,768]{1,0:T(8,128)}, u32[]{:S(2)}) copy-start(f32[256,768]{1,0:T(8,128)} %get-tuple-element.43) | copy-start | bytes 2359300
  231.9 10.7 %all-to-all-start.2 = ((bf16[2,2,49152]{2,1,0:T(2,128)(2,1)}), bf16[2,2,49152]{2,1,0:T(2,128)(2,1)S(1)}, u32[]{:S(2)}, u32[]{:S(2)}) async-start(bf16[2,2,49152]{2,1,0:T(2,128)(2,1)} %reshape.788), calls=%async_computation.2 | async-start | bytes 786432 | tf_op jit(solution)/shard_map/all_to_all | solution.py:167
  242.6 16.3 %all-to-all-start.4 = ((f32[1,256,768]{2,0,1:T(1,128)}), f32[1,256,768]{2,0,1:T(1,128)S(1)}, u32[]{:S(2)}, u32[]{:S(2)}) async-start(f32[1,256,768]{2,0,1:T(1,128)} %copy.70), calls=%async_computation.4 | async-start | bytes 1572864 | tf_op jit(solution)/shard_map/all_to_all | solution.py:219
  303.2 70.2 %copy-start.15 = (bf16[2,768]{1,0:T(2,128)(2,1)S(1)}, bf16[2,768]{1,0:T(2,128)(2,1)}, u32[]{:S(2)}) copy-start(bf16[2,768]{1,0:T(2,128)(2,1)} %param.15) | copy-start | bytes 9220
  361.1 11.0 %all-to-all-start.5 = ((f32[16,1,96]{2,1,0:T(1,128)}), f32[16,1,96]{2,1,0:T(1,128)S(1)}, u32[]{:S(2)}, u32[]{:S(2)}) async-start(f32[16,1,96]{2,1,0:T(1,128)} %bitcast.31), calls=%async_computation.5 | async-start | bytes 16384 | tf_op jit(solution)/shard_map/all_to_all | solution.py:257
Sparse Core Ops, SparseCore 0:
  10.3 55.3 all-gather.6
  68.0 40.5 all-gather.8
  110.9 53.7 all-gather.10
  206.2 95.5 reduce-scatter.6
  305.1 53.6 all-gather.12
  364.1 102.3 reduce-scatter.4
  471.9 106.5 reduce-scatter.8
  584.0 106.4 reduce-scatter.10
